TPU v7x, 512 devices: a whole 4x4x16 slice. The times are simulated.
512 devices in a mesh: lon: 8 (over y, core), lat: 16 (over z), depth: 4 (over x).
Axes of the slice: x: 4, y: 4, z: 16, core: 2. Of those that a mesh axis runs over, the one named last changes fastest.
Arguments:
- snapshots: float32 [524288, 256], P(('lon', 'lat', 'depth')), may hold values from -300 to 300
- live_rows: int32 [512], P(('lon', 'lat', 'depth')), may hold values from 128 to 1024, as said below
- column_order: int32 [256], replicated, may hold values from 0 to 255, each once
Outputs:
- snapshot_basis: float32 [524288, 256], P(('lon', 'lat', 'depth'))
- triangular: float32 [256, 256], replicated
- highpass: float32 [524288, 256], P(('lon', 'lat', 'depth'))
Inputs may be any that keep to these rules, and one draw needn't show every extreme that they name: `live_rows`: each entry is a multiple of 128; some block has all 1024 rows live and some other block has 128.
All inputs are finite; a program needn't handle non-finite values.
Results may differ from a plain program's by a relative error of at most 0.00005.
Values sent between devices are 32-bit elements; how exact they have to be, the bound alone decides.
A program may use at most 64 MiB of HBM per device.

v0:
```python
import jax
import jax.numpy as jnp
from jax import lax
from jax.sharding import PartitionSpec as P

LOW = 32


def on_device(snapshots, live_rows, column_order):
    row_count = snapshots.shape[0]
    total_rows = row_count * lax.axis_size("lon") * lax.axis_size("lat") * lax.axis_size("depth")
    picked = jnp.take(snapshots, column_order, axis=1)
    live_mask = (lax.iota(jnp.int32, row_count) < live_rows[0])[:, None]
    masked = jnp.where(live_mask, picked, jnp.zeros_like(picked))
    local_gram = (
        lax.dot_general(masked, masked, (((0,), (0,)), ((), ())), precision=lax.Precision.HIGHEST)
        / total_rows
    )
    global_gram = lax.psum(local_gram, ("lon", "lat", "depth"))
    lower_factor = jnp.linalg.cholesky(global_gram)
    triangular = lower_factor.T
    snapshot_basis = jax.scipy.linalg.solve_triangular(lower_factor, masked.T, lower=True).T
    highpass = masked - jnp.dot(
        snapshot_basis[:, :LOW], triangular[:LOW, :], precision=lax.Precision.HIGHEST
    )
    return (snapshot_basis, triangular, highpass)


def solution(mesh):
    placed = (P(("lon", "lat", "depth"), None), P(("lon", "lat", "depth")), P())
    return jax.shard_map(
        on_device,
        mesh=mesh,
        in_specs=placed,
        out_specs=(P(("lon", "lat", "depth"), None), P(), P(("lon", "lat", "depth"), None)),
        check_vma=False,
    )
```

profile of v0, /device:TPU:2, one launch (start us, length us, event | category | flops | bytes accessed | tf_op | source)
XLA Modules:
  0.0 559.2 jit_solution(3424189647287764068)
XLA Ops:
  7.2 0.0 copy-start.1
  7.2 0.0 all-reduce.3.cloned.1.call-start
  7.2 0.7 compare_select_fusion
  7.9 1.6 copy.6
  9.5 1.1 gather_fusion
  10.6 0.3 copy.7
  11.6 0.2 select_select_fusion
  11.8 2.5 convolution_multiply_fusion
  14.3 0.0 all-reduce.3.cloned.1.call-update
  14.4 470.3 %all-reduce.3.cloned.1.call-done = f32[256,256]{0,1:T(8,128)} async-done(((f32[256,256]{0,1:T(8,128)}), f32[256,256]{0,1:T(8,128)}) %all-reduce.3.cloned.1.call-update) | async-done | bytes 262160 | tf_op jit(solution)/shard_map/psum | solution.py:19
  484.7 1.1 copy.9
  485.9 11.7 %cholesky.50 = f32[128,128]{1,0:T(8,128)S(1)} custom-call(f32[128,128]{1,0:T(8,128)S(1)} %cholesky.118), custom_call_target="Cholesky" | custom-call | tf_op jit(solution)/shard_map/jit(cholesky)/cholesky | solution.py:20
  497.7 9.8 %custom-call.15 = f32[1,128,128]{1,2,0:T(8,128)S(1)} custom-call(f32[1,128,128]{2,1,0:T(8,128)S(1)} %get-tuple-element.29), custom_call_target="InvertDiagBlocksLowerTriangular" | custom-call | tf_op jit(solution)/shard_map/jit(cholesky)/cholesky | solution.py:20
  507.5 0.3 fusion.9
  507.8 0.1 copy.10
  507.9 0.3 convolution_subtract_fusion.2
  508.2 11.9 %cholesky.105 = f32[128,128]{1,0:T(8,128)S(1)} custom-call(f32[128,128]{1,0:T(8,128)S(1)} %convolution_subtract_fusion.2), custom_call_target="Cholesky" | custom-call | tf_op jit(solution)/shard_map/jit(cholesky)/cholesky | solution.py:20
  520.1 0.6 compare_reduce_fusion
  522.1 0.1 triangular_solve.60
  522.2 4.0 while.1
  522.2 0.6 fusion.20
  522.8 1.4 bitcast_dynamic-update-slice_fusion.2
  524.2 0.6 fusion.20
  524.8 1.4 bitcast_dynamic-update-slice_fusion.2
  526.2 19.7 %custom-call.16 = f32[2,128,128]{1,2,0:T(8,128)S(1)} custom-call(f32[2,128,128]{2,1,0:T(8,128)S(1)} %get-tuple-element.10), custom_call_target="InvertDiagBlocksLowerTriangular" | custom-call | tf_op jit(solution)/shard_map/jit(_solve_triangular)/triangular_solve | solution.py:22
  545.8 0.6 fusion
  546.5 1.0 convolution_subtract_fusion.1
  547.5 0.6 fusion.8
  548.1 0.1 maximum_bitcast_fusion
  548.2 1.3 copy.11
  549.6 2.0 convolution_subtract_fusion
  551.6 0.8 copy.12
  (17 shorter events, 0.2 us)
Async XLA Ops:
  7.2 0.8 copy-start.1
  7.2 477.5 %all-reduce.3.cloned.1.call-start = ((), (), s32[]{:S(2)}) async-start(), calls=%async_computation | async-start | bytes 524288 | tf_op jit(solution)/shard_map/psum | solution.py:19
  484.7 1.2 copy-start
Sparse Core Ops, SparseCore 0:
  14.5 470.1 all-reduce.2
where the time goes:
time: 559 us
  waiting for transfers between devices  470 us (84%)
  other arithmetic  54.9 us (10%)
  between operations  16.2 us (3%)
  local copies, waits for them, and re-layouts  10.4 us (2%)
  matrix products  7.37 us (1%)
    psum x1, waiting for transfers between devices, on_device(): global_gram = lax.psum(local_gram, ('lon', 'lat', 'depth'))  470 us
    another operation x6, other arithmetic, on_device(): lower_factor = jnp.linalg.cholesky(global_gram)  34.1 us
    another operation x2, other arithmetic, on_device(): jax.scipy.linalg.solve_triangular(lower_factor, masked.T, lower=True)  19.7 us
  transfers between devices with their start and end apart: 1, of which 1 were waited for; matrix products, arithmetic and copies ran while one was open for 0% of the time, Pallas kernels for 0%

commit v1 on v0

--- a/solution.py
+++ b/solution.py
@@ -16,7 +16,7 @@
         lax.dot_general(masked, masked, (((0,), (0,)), ((), ())), precision=lax.Precision.HIGHEST)
         / total_rows
     )
-    global_gram = lax.psum(local_gram, ("lon", "lat", "depth"))
+    global_gram = lax.psum(lax.psum(local_gram, "lon"), ("lat", "depth"))
     lower_factor = jnp.linalg.cholesky(global_gram)
     triangular = lower_factor.T
     snapshot_basis = jax.scipy.linalg.solve_triangular(lower_factor, masked.T, lower=True).T

time: 559 us -> 439 us (0.79)
  the two profiles are of different devices: /device:TPU:2 before, /device:TPU:8 now
where the time goes in v1:
time: 439 us
  waiting for transfers between devices  349 us (79%)
  other arithmetic  54.7 us (12%)
  between operations  16.2 us (4%)
  local copies, waits for them, and re-layouts  10.4 us (2%)
  matrix products  7.37 us (2%)
    psum x2, waiting for transfers between devices, on_device(): global_gram = lax.psum(lax.psum(local_gram, 'lon'), ('lat', 'depth'))  349 us
    another operation x6, other arithmetic, on_device(): lower_factor = jnp.linalg.cholesky(global_gram)  33.9 us
    another operation x2, other arithmetic, on_device(): jax.scipy.linalg.solve_triangular(lower_factor, masked.T, lower=True)  19.7 us
  transfers between devices with their start and end apart: 2, of which 2 were waited for; matrix products, arithmetic and copies ran while one was open for 0% of the time, Pallas kernels for 0%

profile of v1, /device:TPU:8, one launch (start us, length us, event | category | flops | bytes accessed | tf_op | source)
XLA Modules:
  0.0 438.5 jit_solution(18401360516119858903)
XLA Ops:
  7.2 0.0 all-reduce.4.cloned.1.call-start
  7.2 0.7 compare_select_fusion
  7.9 1.6 copy.6
  9.5 1.1 gather_fusion
  10.6 0.3 copy.7
  11.6 0.2 select_select_fusion
  11.8 2.5 convolution_multiply_fusion
  14.3 0.2 all-reduce.6.cloned.1.call-start
  14.6 77.9 %all-reduce.4.cloned.1.call-done = f32[256,256]{0,1:T(8,128)} async-done(((f32[256,256]{0,1:T(8,128)}), f32[256,256]{0,1:T(8,128)}) %all-reduce.4.cloned.1.call-update) | async-done | bytes 262160 | tf_op jit(solution)/shard_map/psum | solution.py:19
  92.5 271.5 %all-reduce.6.cloned.1.call-done = f32[256,256]{0,1:T(8,128)} async-done(((f32[256,256]{0,1:T(8,128)}), f32[256,256]{0,1:T(8,128)}) %all-reduce.6.cloned.1.call-update) | async-done | bytes 262160 | tf_op jit(solution)/shard_map/psum | solution.py:19
  364.0 1.1 copy.9
  365.2 11.7 %cholesky.50 = f32[128,128]{1,0:T(8,128)S(1)} custom-call(f32[128,128]{1,0:T(8,128)S(1)} %cholesky.118), custom_call_target="Cholesky" | custom-call | tf_op jit(solution)/shard_map/jit(cholesky)/cholesky | solution.py:20
  376.9 9.8 %custom-call.15 = f32[1,128,128]{1,2,0:T(8,128)S(1)} custom-call(f32[1,128,128]{2,1,0:T(8,128)S(1)} %get-tuple-element.29), custom_call_target="InvertDiagBlocksLowerTriangular" | custom-call | tf_op jit(solution)/shard_map/jit(cholesky)/cholesky | solution.py:20
  386.8 0.3 fusion.9
  387.1 0.1 copy.10
  387.2 0.3 convolution_subtract_fusion.2
  387.5 11.7 %cholesky.105 = f32[128,128]{1,0:T(8,128)S(1)} custom-call(f32[128,128]{1,0:T(8,128)S(1)} %convolution_subtract_fusion.2), custom_call_target="Cholesky" | custom-call | tf_op jit(solution)/shard_map/jit(cholesky)/cholesky | solution.py:20
  399.2 0.6 compare_reduce_fusion
  401.2 0.1 triangular_solve.60
  401.3 4.2 while.1
  401.5 0.6 fusion.20
  402.1 1.4 bitcast_dynamic-update-slice_fusion.2
  403.5 0.6 fusion.20
  404.1 1.4 bitcast_dynamic-update-slice_fusion.2
  405.5 19.7 %custom-call.16 = f32[2,128,128]{1,2,0:T(8,128)S(1)} custom-call(f32[2,128,128]{2,1,0:T(8,128)S(1)} %get-tuple-element.10), custom_call_target="InvertDiagBlocksLowerTriangular" | custom-call | tf_op jit(solution)/shard_map/jit(_solve_triangular)/triangular_solve | solution.py:22
  425.2 0.6 fusion
  425.8 1.0 convolution_subtract_fusion.1
  426.8 0.6 fusion.8
  427.4 0.1 maximum_bitcast_fusion
  427.6 1.3 copy.11
  428.9 2.0 convolution_subtract_fusion
  430.9 0.8 copy.12
  (20 shorter events, 0.3 us)
Async XLA Ops:
  7.2 0.8 copy-start.1
  7.2 85.3 %all-reduce.4.cloned.1.call-start = ((), (), s32[]{:S(2)}) async-start(), calls=%async_computation | async-start | bytes 524288 | tf_op jit(solution)/shard_map/psum | solution.py:19
  14.3 349.6 %all-reduce.6.cloned.1.call-start = ((), (), s32[]{:S(2)}) async-start(), calls=%async_computation.1 | async-start | bytes 524288 | tf_op jit(solution)/shard_map/psum | solution.py:19
  364.0 1.2 copy-start
Sparse Core Ops, SparseCore 0:
  14.5 77.9 all-reduce.3
  95.9 268.0 all-reduce.5
